TPU v7x, 512 devices: a whole 4x8x8 slice. The times are simulated.
512 devices in a mesh: blk: 32 (over z_lo, y, core), rows: 16 (over x, z_hi).
Axes of the slice: x: 4, y: 8, z: 8 (z_hi: 4, z_lo: 2; z = z_hi * 2 + z_lo), core: 2. Of those that a mesh axis runs over, the one named last changes fastest.
Arguments:
- covariance: float32 [16384, 2, 32, 256], P('rows', None, 'blk'), may hold values from 0 to 5, as said below
- panel_order: int32 [64], replicated, may hold values from 0 to 63, each once
Outputs:
- factored: float32 [16384, 2, 32, 256], P('rows', None, 'blk')
Inputs may be any that keep to these rules, and one draw needn't show every extreme that they name: covariance is symmetric and positive definite. `panel_order`: every panel appears once; panel j is held by index j % 32 of blk.
All inputs are finite; a program needn't handle non-finite values.
Results may differ from a plain program's by a relative error of at most 0.0003.
Values sent between devices are 32-bit elements; how exact they have to be, the bound alone decides.
No kernel may reach another device: no remote copies, remote signals or barrier semaphores. Data moves between devices by JAX's collectives and lax.ppermute only.
A program may use at most 64 MiB of HBM per device.

v0:
```python
import jax
import jax.numpy as jnp
from jax import lax
from jax.sharding import PartitionSpec as P

SECTIONS = 2


def padded_to(lines, size):
    spare = -lines.shape[0] % size
    if not spare:
        return lines
    return jnp.concatenate([lines, jnp.zeros((spare, *lines.shape[1:]), lines.dtype)])


def broadcast_by_parts(array, axis, root):
    lines = jnp.where(lax.axis_index(axis) == root, array, jnp.zeros_like(array)).reshape(
        -1, *array.shape[1:][-1:]
    )
    padded = padded_to(lines, lax.axis_size(axis))
    own = lax.psum_scatter(padded, axis, scatter_dimension=0, tiled=True)
    return lax.all_gather(own, axis, axis=0, tiled=True)[: len(lines)].reshape(array.shape)


def from_root(array, axis, root):
    return lax.dynamic_index_in_dim(lax.all_gather(array, axis), root, 0, keepdims=False)


def inverse_factor(diagonal_block):
    lower_factor = jnp.linalg.cholesky(diagonal_block)
    identity_block = jnp.eye(diagonal_block.shape[0], dtype=diagonal_block.dtype)
    return lax.linalg.triangular_solve(lower_factor, identity_block, left_side=True, lower=True)


def product(first_matrix, second_matrix):
    return jnp.dot(
        first_matrix,
        second_matrix,
        precision=lax.Precision.HIGHEST,
        preferred_element_type=jnp.float32,
    )


def local(covariance, panel_order):
    row_count = covariance.shape[0]
    slot_count = covariance.shape[1]
    panel_width = covariance.shape[3]
    owner_count = lax.axis_size("blk")
    column_index = lax.axis_index("blk")
    row_index = lax.axis_index("rows")
    working = covariance.reshape(row_count, slot_count, panel_width)
    identity_block = jnp.eye(panel_width, dtype=jnp.float32)
    slot_panels = jnp.arange(slot_count, dtype=jnp.int32) * owner_count + column_index
    for round_index in range(SECTIONS):
        target = panel_order[round_index]
        owner_column = target % owner_count
        slot_here = target // owner_count
        first_column = target * panel_width
        root_row = first_column // row_count
        offset = first_column % row_count
        finished = jnp.any(slot_panels[:, None] == panel_order[None, : round_index + 1], axis=1)
        target_slot = slot_panels == target
        live_weight = jnp.where(finished, 0.0, 1.0).astype(jnp.float32)
        local_panel = lax.dynamic_index_in_dim(working, slot_here, 1, keepdims=False)
        received_panel = broadcast_by_parts(local_panel, "blk", owner_column)
        diagonal_block = lax.dynamic_slice_in_dim(received_panel, offset, panel_width, 0)
        diagonal_block = jnp.where(row_index == root_row, diagonal_block, identity_block)
        inverse = inverse_factor(diagonal_block)
        across = lax.dynamic_slice_in_dim(working, offset, panel_width, 0).reshape(
            panel_width, slot_count * panel_width
        )
        solved = product(inverse.T, product(inverse, across)).reshape(
            panel_width, slot_count, panel_width
        )
        solved = jnp.where(
            target_slot[None, :, None], inverse.T[:, None, :], solved * live_weight[None, :, None]
        )
        solved = from_root(solved, "rows", root_row)
        change = jnp.einsum(
            "rk,kpc->rpc",
            received_panel,
            solved,
            precision=lax.Precision.HIGHEST,
            preferred_element_type=jnp.float32,
        )
        working = jnp.where(target_slot[None, :, None], change, working - change)
    return working.reshape(row_count, slot_count, 1, panel_width)


def solution(mesh):
    return jax.shard_map(
        local,
        mesh=mesh,
        in_specs=(P("rows", None, "blk", None), P()),
        out_specs=P("rows", None, "blk", None),
        check_vma=False,
    )
```

profile of v0, /device:TPU:2, one launch (start us, length us, event | category | flops | bytes accessed | tf_op | source)
XLA Modules:
  0.0 798.6 jit_solution(15428723638569665150)
XLA Ops:
  6.5 1.3 fusion.42
  10.4 1.9 constant_dynamic-slice_fusion.5
  12.4 1.3 copy.57
  13.8 1.3 copy.53
  15.2 125.6 %reduce-scatter.7.cloned.1.call-done = f32[32,256]{1,0:T(8,128)} async-done(((f32[1024,256]{1,0:T(8,128)}), f32[32,256]{1,0:T(8,128)}) %reduce-scatter.7.cloned.1.call-update) | async-done | bytes 32784 | tf_op jit(solution)/shard_map/reduce_scatter | solution.py:21
  141.6 1.6 dynamic-slice_reduce_fusion
  143.9 60.9 %all-gather.5.cloned.1.call-done = f32[1024,256]{1,0:T(8,128)} async-done(((f32[32,256]{1,0:T(8,128)}), f32[1024,256]{1,0:T(8,128)}) %all-gather.5.cloned.1.call-update) | async-done | bytes 1048592 | tf_op jit(solution)/shard_map/all_gather | solution.py:22
  204.8 1.0 constant_dynamic-slice_fusion.4
  205.9 0.8 copy.35
  206.8 1.0 fusion.10
  207.8 0.7 copy-done.3
  208.5 11.7 %cholesky.130 = f32[128,128]{1,0:T(8,128)S(1)} custom-call(f32[128,128]{1,0:T(8,128)S(1)} %cholesky.194), custom_call_target="Cholesky" | custom-call | tf_op jit(solution)/shard_map/jit(cholesky)/cholesky | solution.py:30
  220.2 9.8 %custom-call.13 = f32[1,128,128]{1,2,0:T(8,128)S(1)} custom-call(f32[1,128,128]{2,1,0:T(8,128)S(1)} %get-tuple-element.52), custom_call_target="InvertDiagBlocksLowerTriangular" | custom-call | tf_op jit(solution)/shard_map/jit(cholesky)/cholesky | solution.py:30
  230.1 1.0 constant_dynamic-update-slice_fusion.1
  231.1 1.1 convolution_subtract_fusion.3
  232.2 12.2 %cholesky.147 = f32[128,128]{1,0:T(8,128)S(1)} custom-call(f32[128,128]{1,0:T(8,128)S(1)} %convolution_subtract_fusion.3), custom_call_target="Cholesky" | custom-call | tf_op jit(solution)/shard_map/jit(cholesky)/cholesky | solution.py:30
  244.4 0.7 compare_reduce_fusion.2
  246.6 4.0 while.4
  247.2 1.4 bitcast_dynamic-update-slice_fusion.4
  249.2 1.4 bitcast_dynamic-update-slice_fusion.4
  250.5 19.7 %custom-call.14 = f32[2,128,128]{1,2,0:T(8,128)S(1)} custom-call(f32[2,128,128]{2,1,0:T(8,128)S(1)} %get-tuple-element.21), custom_call_target="InvertDiagBlocksLowerTriangular" | custom-call | tf_op jit(solution)/shard_map/triangular_solve/custom-call.0 | solution.py:32
  271.3 0.7 fusion.19
  273.3 1.8 copy.37
  275.4 1.9 fusion.6
  279.6 4.4 copy.40
  284.1 116.5 %all-gather.7.cloned.1.call-done = f32[16,256,2,256]{3,1,2,0:T(8,128)} async-done(((f32[1,256,2,256]{3,1,2,0:T(8,128)}), f32[16,256,2,256]{3,1,2,0:T(8,128)}) %all-gather.7.cloned.1.call-update) | async-done | bytes 8388624 | tf_op jit(solution)/shard_map/all_gather | solution.py:26
  400.6 3.7 subtract_select_fusion.1
  404.4 1.3 copy.55
  405.8 118.6 %reduce-scatter.9.cloned.1.call-done = f32[32,256]{1,0:T(8,128)} async-done(((f32[1024,256]{1,0:T(8,128)}), f32[32,256]{1,0:T(8,128)}) %reduce-scatter.9.cloned.1.call-update) | async-done | bytes 32784 | tf_op jit(solution)/shard_map/reduce_scatter | solution.py:21
  526.1 62.1 %all-gather.9.cloned.1.call-done = f32[1024,256]{1,0:T(8,128)} async-done(((f32[32,256]{1,0:T(8,128)}), f32[1024,256]{1,0:T(8,128)}) %all-gather.9.cloned.1.call-update) | async-done | bytes 1048592 | tf_op jit(solution)/shard_map/all_gather | solution.py:22
  588.2 1.0 constant_dynamic-slice_fusion.3
  589.3 0.8 copy.43
  590.2 1.0 fusion.9
  591.2 0.7 copy-done.2
  591.9 11.7 %cholesky.164 = f32[128,128]{1,0:T(8,128)S(1)} custom-call(f32[128,128]{1,0:T(8,128)S(1)} %cholesky.197), custom_call_target="Cholesky" | custom-call | tf_op jit(solution)/shard_map/jit(cholesky)/cholesky | solution.py:30
  603.6 0.6 compare_reduce_fusion.1
  604.3 9.8 %custom-call.15 = f32[1,128,128]{1,2,0:T(8,128)S(1)} custom-call(f32[1,128,128]{2,1,0:T(8,128)S(1)} %get-tuple-element.48), custom_call_target="InvertDiagBlocksLowerTriangular" | custom-call | tf_op jit(solution)/shard_map/jit(cholesky)/cholesky | solution.py:30
  614.1 1.0 constant_dynamic-update-slice_fusion
  615.2 1.1 convolution_subtract_fusion.2
  616.3 11.7 %cholesky.181 = f32[128,128]{1,0:T(8,128)S(1)} custom-call(f32[128,128]{1,0:T(8,128)S(1)} %convolution_subtract_fusion.2), custom_call_target="Cholesky" | custom-call | tf_op jit(solution)/shard_map/jit(cholesky)/cholesky | solution.py:30
  629.9 4.0 while.5
  630.8 1.3 bitcast_dynamic-update-slice_fusion.5
  632.7 1.3 bitcast_dynamic-update-slice_fusion.5
  634.0 19.7 %custom-call.16 = f32[2,128,128]{1,2,0:T(8,128)S(1)} custom-call(f32[2,128,128]{2,1,0:T(8,128)S(1)} %get-tuple-element.22), custom_call_target="InvertDiagBlocksLowerTriangular" | custom-call | tf_op jit(solution)/shard_map/triangular_solve/custom-call.0 | solution.py:32
  656.5 0.9 fusion.5
  657.4 123.3 %all-gather.11.cloned.1.call-done = f32[16,256,2,256]{3,1,2,0:T(8,128)} async-done(((f32[1,256,2,256]{3,1,2,0:T(8,128)}), f32[16,256,2,256]{3,1,2,0:T(8,128)}) %all-gather.11.cloned.1.call-update) | async-done | bytes 8388624 | tf_op jit(solution)/shard_map/all_gather | solution.py:26
  780.8 4.7 fusion
  785.5 6.0 copy.49
  (71 shorter events, 11.3 us)
Async XLA Ops:
  6.5 134.3 %reduce-scatter.7.cloned.1.call-start = ((), (), s32[]{:S(2)}) async-start(), calls=%async_computation.6 | async-start | bytes 1081344 | tf_op jit(solution)/shard_map/reduce_scatter | solution.py:21
  13.8 127.7 %copy-start = (f32[1024,2,1,256]{3,2,1,0:T(1,128)S(1)}, f32[1024,2,1,256]{3,2,1,0:T(1,128)}, u32[]{:S(2)}) copy-start(f32[1024,2,1,256]{3,2,1,0:T(1,128)} %param.5) | copy-start | bytes 6291460
  15.2 189.6 %all-gather.5.cloned.1.call-start = ((), (), s32[]{:S(2)}) async-start(), calls=%async_computation.2 | async-start | bytes 1081344 | tf_op jit(solution)/shard_map/all_gather | solution.py:22
  140.9 259.7 %all-gather.7.cloned.1.call-start = ((), (), s32[]{:S(2)}) async-start(), calls=%async_computation.3 | async-start | bytes 8912896 | tf_op jit(solution)/shard_map/all_gather | solution.py:26
  207.8 0.7 copy-start.3
  277.3 247.1 %reduce-scatter.9.cloned.1.call-start = ((), (), s32[]{:S(2)}) async-start(), calls=%async_computation.7 | async-start | bytes 1081344 | tf_op jit(solution)/shard_map/reduce_scatter | solution.py:21
  279.6 121.0 %copy-start.1 = (f32[1024,256]{1,0:T(8,128)S(1)}, f32[1024,256]{1,0:T(8,128)}, u32[]{:S(2)}) copy-start(f32[1024,256]{1,0:T(8,128)} %all-gather.5.cloned.1.call-done) | copy-start | bytes 3145732
  404.4 121.4 %copy-start.4 = (s32[64]{0:T(128)S(1)}, s32[64]{0:T(128)}, u32[]{:S(2)}) copy-start(s32[64]{0:T(128)} %param.6) | copy-start | bytes 772
  405.8 182.4 %all-gather.9.cloned.1.call-start = ((), (), s32[]{:S(2)}) async-start(), calls=%async_computation.4 | async-start | bytes 1081344 | tf_op jit(solution)/shard_map/all_gather | solution.py:22
  524.4 256.3 %all-gather.11.cloned.1.call-start = ((), (), s32[]{:S(2)}) async-start(), calls=%async_computation.5 | async-start | bytes 8912896 | tf_op jit(solution)/shard_map/all_gather | solution.py:26
  591.2 0.7 copy-start.2
Sparse Core Ops, SparseCore 0:
  15.3 125.5 reduce-scatter.6
  143.0 61.7 all-gather.4
  277.4 123.1 all-gather.6
  405.9 118.4 reduce-scatter.8
  526.4 61.7 all-gather.8
  657.6 123.1 all-gather.10
where the time goes:
time: 809 us; the launch traced here: 799 us
  waiting for transfers between devices  607 us (75%)
  other arithmetic  116 us (14%)
  local copies, waits for them, and re-layouts  35 us (4%)
  between operations  22.8 us (3%)
  matrix products  17.2 us (2%)
    reduce_scatter x2, waiting for transfers between devices, broadcast_by_parts(): own = lax.psum_scatter(padded, axis, scatter_dimension=0, tiled=True)  244 us
    all_gather x2, waiting for transfers between devices, from_root(): lax.all_gather(array, axis)  240 us
    all_gather x2, waiting for transfers between devices, broadcast_by_parts(): lax.all_gather(own, axis, axis=0, tiled=True)[:len(lines)]  123 us
    another operation x13, other arithmetic, inverse_factor(): lower_factor = jnp.linalg.cholesky(diagonal_block)  69 us
    another operation x5, other arithmetic, inverse_factor(): lax.linalg.triangular_solve(lower_factor, identity_block, left_side=True,...  39.4 us
  transfers between devices with their start and end apart: 6, of which 6 were waited for; matrix products, arithmetic and copies ran while one was open for 1% of the time, Pallas kernels for 0%

commit v1 on v0

--- a/solution.py
+++ b/solution.py
@@ -19,7 +19,9 @@
     )
     padded = padded_to(lines, lax.axis_size(axis))
     own = lax.psum_scatter(padded, axis, scatter_dimension=0, tiled=True)
-    return lax.all_gather(own, axis, axis=0, tiled=True)[: len(lines)].reshape(array.shape)
+    return jnp.concatenate(
+        lax.all_to_all(jnp.stack([own] * lax.axis_size(axis)), axis, 0, 0), axis=0
+    )[: len(lines)].reshape(array.shape)
 
 
 def from_root(array, axis, root):

time: 809 us -> 777 us (0.960)
  waiting for transfers between devices: 607 us -> 530 us
  local copies, waits for them, and re-layouts: 35 us -> 52.4 us
  other arithmetic: 116 us -> 128 us
    all_gather x2 -> x0, waiting for transfers between devices: 123 us -> none  [broadcast_by_parts(): lax.all_gather(own, axis, axis=0, tiled=True)[:len(lines)]]
    all_to_all x0 -> x2, waiting for transfers between devices: none -> 50.4 us  [broadcast_by_parts(): lax.all_to_all(jnp.stack([own] * lax.axis_size(axis)), axis, 0, 0)]
where the time goes in v1:
time: 777 us; the launch traced here: 766 us
  waiting for transfers between devices  530 us (68%)
  other arithmetic  128 us (16%)
  local copies, waits for them, and re-layouts  52.4 us (7%)
  matrix products  23.6 us (3%)
  between operations  22.9 us (3%)
  starting transfers between devices  8.16 us (1%)
    reduce_scatter x2, waiting for transfers between devices, broadcast_by_parts(): own = lax.psum_scatter(padded, axis, scatter_dimension=0, tiled=True)  244 us
    all_gather x2, waiting for transfers between devices, from_root(): lax.all_gather(array, axis)  235 us
    another operation x13, other arithmetic, inverse_factor(): lower_factor = jnp.linalg.cholesky(diagonal_block)  71.6 us
    all_to_all x2, waiting for transfers between devices, broadcast_by_parts(): lax.all_to_all(jnp.stack([own] * lax.axis_size(axis)), axis, 0, 0)  50.4 us
    another operation x5, other arithmetic, inverse_factor(): lax.linalg.triangular_solve(lower_factor, identity_block, left_side=True,...  44.3 us
  transfers between devices with their start and end apart: 6, of which 6 were waited for; matrix products, arithmetic and copies ran while one was open for 1% of the time, Pallas kernels for 0%

profile of v1, /device:TPU:2, one launch (start us, length us, event | category | flops | bytes accessed | tf_op | source)
XLA Modules:
  0.0 765.5 jit_solution(1754476759122427524)
XLA Ops:
  6.5 1.3 fusion.40
  10.7 2.1 broadcast_select_fusion
  13.9 125.7 %reduce-scatter.5.cloned.1.call-done = f32[32,256]{1,0:T(8,128)} async-done(((f32[1024,256]{1,0:T(8,128)}), f32[32,256]{1,0:T(8,128)}) %reduce-scatter.5.cloned.1.call-update) | async-done | bytes 32784 | tf_op jit(solution)/shard_map/reduce_scatter | solution.py:21
  139.5 1.8 stack.4
  141.4 3.9 all-to-all-start
  146.1 1.6 dynamic-slice_reduce_fusion
  149.3 24.5 %all-to-all-done = f32[32,32,256]{2,1,0:T(8,128)S(1)} async-done(((f32[32,32,256]{2,1,0:T(8,128)}), f32[32,32,256]{2,1,0:T(8,128)S(1)}, u32[]{:S(2)}, u32[]{:S(2)}) %all-to-all-start) | async-done | bytes 1048608 | tf_op jit(solution)/shard_map/all_to_all | solution.py:23
  174.5 1.8 copy.67
  177.0 1.8 copy.46
  180.5 11.7 %cholesky.130 = f32[128,128]{1,0:T(8,128)S(1)} custom-call(f32[128,128]{1,0:T(8,128)S(1)} %cholesky.194), custom_call_target="Cholesky" | custom-call | tf_op jit(solution)/shard_map/jit(cholesky)/cholesky | solution.py:32
  192.3 10.4 %custom-call.13 = f32[1,128,128]{1,2,0:T(8,128)} custom-call(f32[1,128,128]{2,1,0:T(8,128)S(1)} %get-tuple-element.52), custom_call_target="InvertDiagBlocksLowerTriangular" | custom-call | tf_op jit(solution)/shard_map/jit(cholesky)/cholesky | solution.py:32
  203.4 1.7 constant_dynamic-update-slice_fusion.1
  206.2 12.2 %cholesky.147 = f32[128,128]{1,0:T(8,128)S(1)} custom-call(f32[128,128]{1,0:T(8,128)S(1)} %convolution_subtract_fusion.3), custom_call_target="Cholesky" | custom-call | tf_op jit(solution)/shard_map/jit(cholesky)/cholesky | solution.py:32
  221.0 1.7 select_select_fusion.1
  222.8 5.8 while.4
  223.5 2.3 bitcast_dynamic-update-slice_fusion.4
  226.4 2.2 bitcast_dynamic-update-slice_fusion.4
  229.3 20.5 %custom-call.14 = f32[2,128,128]{1,2,0:T(8,128)S(1)} custom-call(f32[2,128,128]{2,1,0:T(8,128)} %copy-done.4), custom_call_target="InvertDiagBlocksLowerTriangular" | custom-call | tf_op jit(solution)/shard_map/triangular_solve/custom-call.0 | solution.py:34
  252.4 1.7 fusion.16
  254.1 1.4 fusion.15
  255.5 1.8 copy.48
  257.3 2.2 reshape.118
  259.4 2.1 fusion.4
  264.2 4.4 copy.51
  268.6 113.8 %all-gather.3.cloned.1.call-done = f32[16,256,2,256]{3,1,2,0:T(8,128)} async-done(((f32[1,256,2,256]{3,1,2,0:T(8,128)}), f32[16,256,2,256]{3,1,2,0:T(8,128)}) %all-gather.3.cloned.1.call-update) | async-done | bytes 8388624 | tf_op jit(solution)/shard_map/all_gather | solution.py:28
  382.4 3.7 subtract_select_fusion.1
  387.5 118.6 %reduce-scatter.7.cloned.1.call-done = f32[32,256]{1,0:T(8,128)} async-done(((f32[1024,256]{1,0:T(8,128)}), f32[32,256]{1,0:T(8,128)}) %reduce-scatter.7.cloned.1.call-update) | async-done | bytes 32784 | tf_op jit(solution)/shard_map/reduce_scatter | solution.py:21
  506.2 1.8 stack.5
  508.0 3.9 all-to-all-start.1
  514.6 25.9 %all-to-all-done.1 = f32[32,32,256]{2,1,0:T(8,128)S(1)} async-done(((f32[32,32,256]{2,1,0:T(8,128)}), f32[32,32,256]{2,1,0:T(8,128)S(1)}, u32[]{:S(2)}, u32[]{:S(2)}) %all-to-all-start.1) | async-done | bytes 1048608 | tf_op jit(solution)/shard_map/all_to_all | solution.py:23
  541.1 1.8 copy.68
  543.7 1.8 copy.54
  547.2 11.7 %cholesky.164 = f32[128,128]{1,0:T(8,128)S(1)} custom-call(f32[128,128]{1,0:T(8,128)S(1)} %cholesky.197), custom_call_target="Cholesky" | custom-call | tf_op jit(solution)/shard_map/jit(cholesky)/cholesky | solution.py:32
  559.6 10.4 %custom-call.15 = f32[1,128,128]{1,2,0:T(8,128)} custom-call(f32[1,128,128]{2,1,0:T(8,128)S(1)} %get-tuple-element.48), custom_call_target="InvertDiagBlocksLowerTriangular" | custom-call | tf_op jit(solution)/shard_map/jit(cholesky)/cholesky | solution.py:32
  570.7 1.7 constant_dynamic-update-slice_fusion
  573.5 11.7 %cholesky.181 = f32[128,128]{1,0:T(8,128)S(1)} custom-call(f32[128,128]{1,0:T(8,128)S(1)} %convolution_subtract_fusion.2), custom_call_target="Cholesky" | custom-call | tf_op jit(solution)/shard_map/jit(cholesky)/cholesky | solution.py:32
  587.8 1.7 select_select_fusion
  589.5 6.1 while.5
  590.5 2.3 bitcast_dynamic-update-slice_fusion.5
  593.4 2.2 bitcast_dynamic-update-slice_fusion.5
  596.3 20.5 %custom-call.16 = f32[2,128,128]{1,2,0:T(8,128)S(1)} custom-call(f32[2,128,128]{2,1,0:T(8,128)} %copy-done.3), custom_call_target="InvertDiagBlocksLowerTriangular" | custom-call | tf_op jit(solution)/shard_map/triangular_solve/custom-call.0 | solution.py:34
  618.7 1.7 fusion.13
  620.3 1.4 fusion.12
  622.6 2.2 reshape.122
  624.8 2.0 fusion.3
  626.8 121.6 %all-gather.5.cloned.1.call-done = f32[16,256,2,256]{3,1,2,0:T(8,128)} async-done(((f32[1,256,2,256]{3,1,2,0:T(8,128)}), f32[16,256,2,256]{3,1,2,0:T(8,128)}) %all-gather.5.cloned.1.call-update) | async-done | bytes 8388624 | tf_op jit(solution)/shard_map/all_gather | solution.py:28
  748.4 4.4 fusion
  752.7 6.0 copy.60
  (71 shorter events, 28.8 us)
Async XLA Ops:
  6.5 133.0 %reduce-scatter.5.cloned.1.call-start = ((), (), s32[]{:S(2)}) async-start(), calls=%async_computation.4 | async-start | bytes 1081344 | tf_op jit(solution)/shard_map/reduce_scatter | solution.py:21
  13.9 132.2 %copy-start = (f32[1024,2,1,256]{3,2,1,0:T(1,128)S(1)}, f32[1024,2,1,256]{3,2,1,0:T(1,128)}, u32[]{:S(2)}) copy-start(f32[1024,2,1,256]{3,2,1,0:T(1,128)} %param.5) | copy-start | bytes 6291460
  141.4 32.4 %all-to-all-start = ((f32[32,32,256]{2,1,0:T(8,128)}), f32[32,32,256]{2,1,0:T(8,128)S(1)}, u32[]{:S(2)}, u32[]{:S(2)}) async-start(f32[32,32,256]{2,1,0:T(8,128)} %stack.4), calls=%async_computation.1 | async-start | bytes 2097152 | tf_op jit(solution)/shard_map/all_to_all | solution.py:23
  145.3 237.1 %all-gather.3.cloned.1.call-start = ((), (), s32[]{:S(2)}) async-start(), calls=%async_computation.5 | async-start | bytes 8912896 | tf_op jit(solution)/shard_map/all_gather | solution.py:28
  179.8 0.7 copy-start.2
  228.6 0.7 copy-start.4
  261.5 244.6 %reduce-scatter.7.cloned.1.call-start = ((), (), s32[]{:S(2)}) async-start(), calls=%async_computation.7 | async-start | bytes 1081344 | tf_op jit(solution)/shard_map/reduce_scatter | solution.py:21
  387.5 126.0 %copy-start.5 = (s32[64]{0:T(128)S(1)}, s32[64]{0:T(128)}, u32[]{:S(2)}) copy-start(s32[64]{0:T(128)} %param.6) | copy-start | bytes 772
  508.0 32.4 %all-to-all-start.1 = ((f32[32,32,256]{2,1,0:T(8,128)}), f32[32,32,256]{2,1,0:T(8,128)S(1)}, u32[]{:S(2)}, u32[]{:S(2)}) async-start(f32[32,32,256]{2,1,0:T(8,128)} %stack.5), calls=%async_computation.2 | async-start | bytes 2097152 | tf_op jit(solution)/shard_map/all_to_all | solution.py:23
  512.0 236.4 %all-gather.5.cloned.1.call-start = ((), (), s32[]{:S(2)}) async-start(), calls=%async_computation.6 | async-start | bytes 8912896 | tf_op jit(solution)/shard_map/all_gather | solution.py:28
  546.5 0.7 copy-start.1
  595.6 0.7 copy-start.3
Sparse Core Ops, SparseCore 0:
  14.0 125.5 reduce-scatter.4
  261.7 120.6 all-gather.2
  387.7 118.4 reduce-scatter.6
  626.9 121.3 all-gather.4
